TPU v7x, 256 devices: a whole 4x4x8 slice. The times are simulated.
256 devices in a mesh: lat: 32 (over z, x_lo, core), lon: 8 (over x_hi, y).
Axes of the slice: x: 4 (x_hi: 2, x_lo: 2; x = x_hi * 2 + x_lo), y: 4, z: 8, core: 2. Of those that a mesh axis runs over, the one named last changes fastest.
Arguments:
- cells: bfloat16 [384, 256, 256], P('lat', 'lon'), may hold values from -120 to 120
- w_query: bfloat16 [256, 256], replicated, may hold values from -0.375 to 0.375
- w_key: bfloat16 [256, 256], replicated, may hold values from -0.375 to 0.375
- w_value: bfloat16 [256, 256], replicated, may hold values from -0.375 to 0.375
- w_out: bfloat16 [256, 256], replicated, may hold values from -0.375 to 0.375
- grad_out: bfloat16 [384, 256, 256], P('lat', 'lon'), may hold values from -6 to 6
Outputs:
- mixed: bfloat16 [384, 256, 256], P('lat', 'lon')
- grad_cells: float32 [384, 256, 256], P('lat', 'lon')
- grad_wq: float32 [256, 256], replicated
- grad_wk: float32 [256, 256], replicated
- grad_wv: float32 [256, 256], replicated
- grad_wo: float32 [256, 256], replicated
All inputs are finite; a program needn't handle non-finite values.
Results may differ from a plain program's by a relative error of at most 0.004.
The roundings to bfloat16 on the way count: a program that leaves them out, or rounds other values in their place, can miss the bound.
Values may be sent and summed in bfloat16 or wider, within the bound.
A program may use at most 128 MiB of HBM per device.

v0:
```python
import jax
import jax.numpy as jnp
from jax import lax
from jax.sharding import PartitionSpec as P

HEADS = 8
REACH = 6


def passed_along(value, axis, steps):
    count = lax.axis_size(axis)
    pairs = [(source, (source + steps) % count) for source in range(count)]
    return lax.ppermute(value, axis, pairs)


def from_behind(value, axis, steps):
    count = lax.axis_size(axis)
    leading, last = (max(0, -steps), min(count, count - steps))
    return lax.ppermute(value, axis, [(source, source + steps) for source in range(leading, last)])


def padded(cells, sides, width):
    for axis, dim in sides:
        count = lax.axis_size(axis)
        head = lax.slice_in_dim(cells, 0, width, axis=dim)
        tail = lax.slice_in_dim(cells, cells.shape[dim] - width, cells.shape[dim], axis=dim)
        cells = jnp.concatenate(
            [
                lax.ppermute(tail, axis, [(i, (i + 1) % count) for i in range(count)]),
                cells,
                lax.ppermute(head, axis, [((i + 1) % count, i) for i in range(count)]),
            ],
            axis=dim,
        )
    return cells


def window_block(queries, key_vals, grad_heads, valid_rows):
    q_rows, q_cols, model_width = queries.shape
    k_rows, k_cols = (key_vals.shape[0], key_vals.shape[1])
    head_dim = model_width // HEADS
    n_query = q_rows * q_cols
    n_key = k_rows * k_cols
    score_scale = head_dim ** (-0.5)
    row_gap = jnp.arange(k_rows)[None, None, :, None] - jnp.arange(q_rows)[:, None, None, None]
    col_gap = jnp.arange(k_cols)[None, None, None, :] - jnp.arange(q_cols)[None, :, None, None]
    inside = (
        (row_gap >= 0)
        & (row_gap <= 2 * REACH)
        & (col_gap >= 0)
        & (col_gap <= 2 * REACH)
        & valid_rows[None, None, :, None]
    )
    inside = inside.reshape(n_query, n_key)
    query_heads = queries.reshape(n_query, HEADS, head_dim)
    key_heads = key_vals[:, :, :model_width].reshape(n_key, HEADS, head_dim)
    value_heads = key_vals[:, :, model_width:].reshape(n_key, HEADS, head_dim)
    grad_split = grad_heads.reshape(n_query, HEADS, head_dim)
    scores = (
        jnp.einsum("qhe,khe->hqk", query_heads, key_heads, preferred_element_type=jnp.float32)
        * score_scale
    )
    scores = jnp.where(inside[None], scores, -1e30)
    row_max = jnp.max(scores, axis=2, keepdims=True)
    weights = jnp.exp(scores - row_max)
    weights = weights / jnp.sum(weights, axis=2, keepdims=True)
    weights_low = weights.astype(jnp.bfloat16)
    attended = jnp.einsum(
        "hqk,khe->qhe", weights_low, value_heads, preferred_element_type=jnp.float32
    )
    attended = attended.astype(jnp.bfloat16).reshape(q_rows, q_cols, model_width)
    grad_weights = jnp.einsum(
        "qhe,khe->hqk", grad_split, value_heads, preferred_element_type=jnp.float32
    )
    centre = jnp.sum(weights * grad_weights, axis=2, keepdims=True)
    grad_scores = (weights * (grad_weights - centre) * score_scale).astype(jnp.bfloat16)
    grad_query = jnp.einsum(
        "hqk,khe->qhe", grad_scores, key_heads, preferred_element_type=jnp.float32
    )
    grad_key = jnp.einsum(
        "hqk,qhe->khe", grad_scores, query_heads, preferred_element_type=jnp.float32
    )
    grad_value = jnp.einsum(
        "hqk,qhe->khe", weights_low, grad_split, preferred_element_type=jnp.float32
    )
    grad_pair = jnp.concatenate(
        [
            grad_key.reshape(k_rows, k_cols, model_width),
            grad_value.reshape(k_rows, k_cols, model_width),
        ],
        axis=2,
    )
    return (attended, grad_query.reshape(q_rows, q_cols, model_width), grad_pair)


def return_rim(grad_ext):
    folded = grad_ext[:, REACH:-REACH]
    for offset, edge_strip in ((-1, grad_ext[:, :REACH]), (1, grad_ext[:, -REACH:])):
        arrived = passed_along(edge_strip, "lon", offset)
        if offset < 0:
            folded = folded.at[:, -REACH:].add(arrived)
        else:
            folded = folded.at[:, :REACH].add(arrived)
    interior = folded[REACH:-REACH]
    for offset, edge_strip in ((-1, folded[:REACH]), (1, folded[-REACH:])):
        arrived = from_behind(edge_strip, "lat", offset)
        if offset < 0:
            interior = interior.at[-REACH:].add(arrived)
        else:
            interior = interior.at[:REACH].add(arrived)
    return interior


def back_project(gradient, weight):
    return jnp.dot(
        gradient.reshape(-1, weight.shape[0]),
        weight.astype(jnp.float32).T,
        precision=lax.Precision.HIGHEST,
    )


def weight_term(inputs, gradient):
    model_width = gradient.shape[-1]
    return lax.dot_general(
        inputs.reshape(-1, model_width).astype(jnp.float32),
        gradient.reshape(-1, model_width),
        (((0,), (0,)), ((), ())),
        precision=lax.Precision.HIGHEST,
    )


def body(cells, w_query, w_key, w_value, w_out, grad_out):
    lat_rows, lon_cols, model_width = cells.shape
    ext_rows = lat_rows + 2 * REACH
    ext_cols = lon_cols + 2 * REACH
    cells_flat = cells.reshape(-1, model_width)
    queries = jnp.dot(cells_flat, w_query, preferred_element_type=jnp.float32).astype(jnp.bfloat16)
    queries = queries.reshape(lat_rows, lon_cols, model_width)
    w_pair = jnp.concatenate([w_key, w_value], axis=1)
    key_vals = jnp.dot(cells_flat, w_pair, preferred_element_type=jnp.float32).astype(jnp.bfloat16)
    key_vals = key_vals.reshape(lat_rows, lon_cols, 2 * model_width)
    key_ext = padded(key_vals, (("lat", 0), ("lon", 1)), REACH)
    grad_heads = jnp.dot(
        grad_out.reshape(-1, model_width), w_out.T, preferred_element_type=jnp.float32
    ).astype(jnp.bfloat16)
    grad_heads = grad_heads.reshape(lat_rows, lon_cols, model_width)
    lat_total = lat_rows * lax.axis_size("lat")
    lat_index = lax.axis_index("lat") * lat_rows - REACH + jnp.arange(ext_rows, dtype=jnp.int32)
    valid_rows = (lat_index >= 0) & (lat_index < lat_total)
    blocks = 1

    def one_block(block_index, state_all):
        attended_all, query_all, grad_ext = state_all
        attended, grad_query, grad_pair = window_block(queries, key_ext, grad_heads, valid_rows)
        attended_all = attended
        query_all = grad_query
        current = grad_ext
        grad_ext = current + grad_pair
        return (attended_all, query_all, grad_ext)

    initial = (
        jnp.zeros((lat_rows, lon_cols, model_width), jnp.bfloat16),
        jnp.zeros((lat_rows, lon_cols, model_width), jnp.float32),
        jnp.zeros((ext_rows, ext_cols, 2 * model_width), jnp.float32),
    )
    attended, grad_query, grad_ext = lax.fori_loop(0, blocks, one_block, initial)
    attended_flat = attended.reshape(-1, model_width)
    mixed = jnp.dot(attended_flat, w_out, preferred_element_type=jnp.float32).astype(jnp.bfloat16)
    mixed = mixed.reshape(lat_rows, lon_cols, model_width)
    term_out = lax.dot_general(
        attended_flat,
        grad_out.reshape(-1, model_width),
        (((0,), (0,)), ((), ())),
        preferred_element_type=jnp.float32,
    )
    term_query = weight_term(cells, grad_query)
    grad_own = return_rim(grad_ext)
    grad_key = grad_own[:, :, :model_width]
    grad_value = grad_own[:, :, model_width:]
    grad_cells = (
        back_project(grad_query, w_query)
        + back_project(grad_key, w_key)
        + back_project(grad_value, w_value)
    )
    term_key = weight_term(cells, grad_key)
    term_value = weight_term(cells, grad_value)
    totals = lax.psum((term_query, term_key, term_value, term_out), ("lat", "lon"))
    grad_scale = (lat_total * lon_cols * lax.axis_size("lon")) ** (-0.5)
    grad_cells = grad_cells.reshape(lat_rows, lon_cols, model_width)
    return (
        mixed,
        grad_cells,
        totals[0] * grad_scale,
        totals[1] * grad_scale,
        totals[2] * grad_scale,
        totals[3] * grad_scale,
    )


def solution(mesh):
    in_specs = (P("lat", "lon", None), P(), P(), P(), P(), P("lat", "lon", None))
    out_specs = (P("lat", "lon", None), P("lat", "lon", None), P(), P(), P(), P())
    return jax.shard_map(body, mesh=mesh, in_specs=in_specs, out_specs=out_specs, check_vma=False)
```

profile of v0, /device:TPU:1, one launch (start us, length us, event | category | flops | bytes accessed | tf_op | source)
XLA Modules:
  0.0 435.6 jit_solution(5564430850650035866)
XLA Ops:
  7.2 0.9 copy-done
  8.1 1.2 convolution_convert_fusion
  9.4 3.3 collective-permute-start.1
  13.7 1.8 and.99
  15.7 1.5 copy.36
  17.2 1.2 convolution_convert_fusion.3
  18.7 1.0 collective-permute-start.2
  19.7 1.3 convolution_convert_fusion.1
  21.0 4.5 %collective-permute-start.3 = (bf16[24,6,512]{2,0,1:T(8,128)(2,1)S(1)}, bf16[24,6,512]{2,0,1:T(8,128)(2,1)S(1)}, u32[]{:S(2)}, u32[]{:S(2)}) collective-permute-start(bf16[24,6,512]{2,0,1:T(8,128)(2,1)S(1)} %copy.48), channel_id=1, source_target_pairs={{1,0},{2,1},{3,2},{4,3},{5,4},{6,5},{7,6},{0,7},{9,8},{10,9},{11,1... | collective-permute-start | bytes 442376 | tf_op jit(solution)/shard_map/ppermute | solution.py:31
  25.5 0.9 collective-permute-done.2
  27.7 1.1 copy.37
  28.8 1.7 reshape.286
  30.5 1.1 copy.35
  31.6 1.0 reshape.285
  32.6 6.6 %fusion.59 = f32[8,384,1056]{1,2,0:T(8,128)} fusion(bf16[384,8,32]{0,2,1:T(8,128)(2,1)S(1)} %bitcast.87, bf16[1056,8,32]{0,2,1:T(8,128)(2,1)S(1)} %reshape.285), kind=kOutput, calls=%fused_computation.83 | convolution fusion | flops 207618048 | bytes 13713408 | tf_op jit(solution)/shard_map/while/body/eval_jaxpr/qhe,khe->hqk/dot_general | solution.py:72
  39.2 8.6 %fusion.58 = (f32[8,384]{1,0:T(8,128)S(1)}, f32[8,384,1056]{1,2,0:T(8,128)}) fusion(pred[384,1056]{0,1:T(8,128)(4,1)} %copy.36, bf16[384,8,32]{0,2,1:T(8,128)(2,1)S(1)} %bitcast.90, bf16[1056,8,32]{0,2,1:T(8,128)(2,1)S(1)} %copy-done.3), kind=kOutput, calls=%fused_computation.82 | convolution fusion | flops 220595232 | bytes 14131200 | tf_op jit(solution)/shard_map/while/body/eval_jaxpr/sub | solution.py:65
  47.8 19.5 %fusion.13 = f32[8,32,384]{2,1,0:T(8,128)S(1)} fusion(bf16[1056,8,32]{0,2,1:T(8,128)(2,1)S(1)} %copy-done.3, f32[8,384,1056]{1,2,0:T(8,128)} %fusion.59, f32[8,384,1056]{1,2,0:T(8,128)} %get-tuple-element.111, f32[8,384]{1,0:T(8,128)S(1)} %get-tuple-element.110), kind=kOutput, calls=%fused_computation.13 | convolution fusion | flops 230330400 | bytes 26898432 | tf_op jit(solution)/shard_map/while/body/eval_jaxpr/hqk,khe->qhe/dot_general | solution.py:77
  67.3 20.3 %fusion.19 = f32[1056,8,32]{0,2,1:T(8,128)S(1)} fusion(bf16[384,8,32]{0,2,1:T(8,128)(2,1)S(1)} %bitcast.93, f32[8,384,1056]{1,2,0:T(8,128)} %fusion.59, f32[8,384,1056]{1,2,0:T(8,128)} %get-tuple-element.111, f32[8,384]{1,0:T(8,128)S(1)} %get-tuple-element.110), kind=kOutput, calls=%fused_computation.25 | convolution fusion | flops 230330400 | bytes 27242496 | tf_op jit(solution)/shard_map/while/body/eval_jaxpr/hqk,qhe->khe/dot_general | solution.py:80
  87.5 7.0 %fusion.22 = f32[1056,8,32]{0,2,1:T(8,128)S(1)} fusion(bf16[384,8,32]{0,2,1:T(8,128)(2,1)} %bitcast.88, f32[8,384]{1,0:T(8,128)S(1)} %get-tuple-element.110, pred[384,1056]{0,1:T(8,128)(4,1)} %copy.36, bf16[384,8,32]{0,2,1:T(8,128)(2,1)} %bitcast.91, bf16[1056,8,32]{0,2,1:T(8,128)(2,1)} %reshape.286), kind=kOutput, calls=%fused_computation.26 | convolution fusion | flops 431460384 | bytes 2433024 | tf_op jit(solution)/shard_map/while/body/eval_jaxpr/hqk,qhe->khe/dot_general | solution.py:83
  94.6 2.6 reshape.292
  97.1 2.4 copy.39
  99.6 2.6 reshape.291
  102.1 2.4 copy.38
  105.3 5.7 %collective-permute-start.4 = (f32[24,6,512]{2,1,0:T(8,128)}, f32[24,6,512]{2,1,0:T(8,128)}, u32[]{:S(2)}, u32[]{:S(2)}) collective-permute-start(f32[24,6,512]{2,1,0:T(8,128)} %fusion.31), channel_id=1, source_target_pairs={{0,7},{1,0},{2,1},{3,2},{4,3},{5,4},{6,5},{7,6},{8,15},{9,8},{10,9... | collective-permute-start | bytes 884744 | tf_op jit(solution)/shard_map/ppermute | solution.py:13
  111.0 7.3 %fusion.28 = bf16[8,32,384]{2,1,0:T(8,128)(2,1)} fusion(bf16[1056,8,32]{0,2,1:T(8,128)(2,1)S(1)} %reshape.285, f32[8,384]{1,0:T(8,128)S(1)} %get-tuple-element.110, pred[384,1056]{0,1:T(8,128)(4,1)} %copy.36, bf16[384,8,32]{0,2,1:T(8,128)(2,1)} %bitcast.92, bf16[1056,8,32]{0,2,1:T(8,128)(2,1)} %reshape.286), kind=kOutput, calls=%fused_computation.32 | convolution fusion | flops 431558688 | bytes 1892352 | tf_op jit(solution)/shard_map/while/body/eval_jaxpr/hqk,khe->qhe/dot_general | solution.py:68
  118.3 1.1 convolution_bitcast_fusion.2
  119.3 1.8 pad_maximum_fusion.1
  121.1 1.4 fusion.27
  122.5 1.4 fusion.60
  124.0 2.9 scatter-add.14
  126.9 4.8 %collective-permute-done.5 = f32[24,6,512]{2,1,0:T(8,128)} collective-permute-done((f32[24,6,512]{2,1,0:T(8,128)}, f32[24,6,512]{2,1,0:T(8,128)}, u32[]{:S(2)}, u32[]{:S(2)}) %collective-permute-start.5) | collective-permute-done | bytes 294944 | tf_op jit(solution)/shard_map/ppermute | solution.py:13
  131.7 1.2 slice_add_fusion.2
  132.9 3.5 scatter-add.15
  136.4 1.2 fusion.53
  137.6 10.7 %collective-permute-start.6 = (f32[6,32,512]{2,1,0:T(8,128)S(1)}, f32[6,32,512]{2,1,0:T(8,128)S(1)}, u32[]{:S(2)}, u32[]{:S(2)}) collective-permute-start(f32[6,32,512]{2,1,0:T(8,128)S(1)} %get-tuple-element.101), channel_id=1, source_target_pairs={{8,0},{16,8},{24,16},{32,24},{40,32},{48,40},{56,48},{64,56},{72,6... | collective-permute-start | bytes 1179656 | tf_op jit(solution)/shard_map/ppermute | solution.py:19
  148.3 1.9 fusion.61
  150.2 1.9 collective-permute-start.7
  152.2 1.9 convolution_convert_fusion.2
  154.1 1.2 slice.181
  155.3 1.1 fusion.35
  157.0 1.2 convolution_bitcast_fusion
  158.2 1.2 convolution_bitcast_fusion.1
  159.9 1.1 convolution_add_fusion
  161.0 260.2 %all-reduce.3.cloned.1.call-done = (f32[256,256]{0,1:T(8,128)}, f32[256,256]{0,1:T(8,128)}, f32[256,256]{0,1:T(8,128)}, f32[256,256]{0,1:T(8,128)}) async-done(((f32[256,256]{0,1:T(8,128)}, f32[256,256]{0,1:T(8,128)}, f32[256,256]{0,1:T(8,128)}, f32[256,256]{0,1:T(8,128)}), (f32[256,256]{0,1:T(8,128)}, f32[256,256]{0,1:T(8,128)}, f32[256,256]{0,1:T(8,128)}, ...) | async-done | bytes 1048592 | tf_op jit(solution)/shard_map/psum | solution.py:187
  421.3 1.0 broadcast_multiply_fusion.3
  423.1 1.0 broadcast_multiply_fusion.2
  424.9 1.0 broadcast_multiply_fusion.1
  426.7 1.0 broadcast_multiply_fusion
  (49 shorter events, 8.1 us)
Async XLA Ops:
  7.2 0.9 copy-start
  7.2 414.1 %all-reduce.3.cloned.1.call-start = ((), (), s32[]{:S(2)}) async-start(), calls=%async_computation | async-start | bytes 2097152 | tf_op jit(solution)/shard_map/psum | solution.py:187
  9.4 9.1 %collective-permute-start.1 = (bf16[6,32,512]{2,1,0:T(8,128)(2,1)S(1)}, bf16[6,32,512]{2,1,0:T(8,128)(2,1)S(1)}, u32[]{:S(2)}, u32[]{:S(2)}) collective-permute-start(bf16[6,32,512]{2,1,0:T(8,128)(2,1)S(1)} %bitcast.96), channel_id=1, source_target_pairs={{8,0},{16,8},{24,16},{32,24},{40,32},{48,40},{56,48},{64,56},{72,6... | collective-permute-start | bytes 589832 | tf_op jit(solution)/shard_map/ppermute | solution.py:31
  12.6 5.8 %collective-permute-start = (bf16[6,32,512]{2,1,0:T(8,128)(2,1)S(1)}, bf16[6,32,512]{2,1,0:T(8,128)(2,1)S(1)}, u32[]{:S(2)}, u32[]{:S(2)}) collective-permute-start(bf16[6,32,512]{2,1,0:T(8,128)(2,1)S(1)} %bitcast.95), channel_id=1, source_target_pairs={{0,8},{8,16},{16,24},{24,32},{32,40},{40,48},{48,56},{56,64},{64,7... | collective-permute-start | bytes 589832 | tf_op jit(solution)/shard_map/ppermute | solution.py:29
  18.4 20.8 %copy-start.6 = (bf16[384,256]{0,1:T(8,128)(2,1)}, bf16[384,256]{0,1:T(8,128)(2,1)S(1)}, u32[]{:S(2)}) copy-start(bf16[384,256]{0,1:T(8,128)(2,1)S(1)} %convolution_convert_fusion.3) | copy-start | bytes 589828
  18.7 7.7 %collective-permute-start.2 = (bf16[24,6,512]{2,0,1:T(8,128)(2,1)S(1)}, bf16[24,6,512]{2,0,1:T(8,128)(2,1)S(1)}, u32[]{:S(2)}, u32[]{:S(2)}) collective-permute-start(bf16[24,6,512]{2,0,1:T(8,128)(2,1)S(1)} %copy.47), channel_id=1, source_target_pairs={{0,1},{1,2},{2,3},{3,4},{4,5},{5,6},{6,7},{7,0},{8,9},{9,10},{10,1... | collective-permute-start | bytes 442376 | tf_op jit(solution)/shard_map/ppermute | solution.py:29
  20.9 18.2 %copy-start.2 = (bf16[384,256]{0,1:T(8,128)(2,1)}, bf16[384,256]{0,1:T(8,128)(2,1)S(1)}, u32[]{:S(2)}) copy-start(bf16[384,256]{0,1:T(8,128)(2,1)S(1)} %convolution_convert_fusion.1) | copy-start | bytes 589828
  21.0 6.6 %collective-permute-start.3 = (bf16[24,6,512]{2,0,1:T(8,128)(2,1)S(1)}, bf16[24,6,512]{2,0,1:T(8,128)(2,1)S(1)}, u32[]{:S(2)}, u32[]{:S(2)}) collective-permute-start(bf16[24,6,512]{2,0,1:T(8,128)(2,1)S(1)} %copy.48), channel_id=1, source_target_pairs={{1,0},{2,1},{3,2},{4,3},{5,4},{6,5},{7,6},{0,7},{9,8},{10,9},{11,1... | collective-permute-start | bytes 442376 | tf_op jit(solution)/shard_map/ppermute | solution.py:31
  31.6 7.6 %copy-start.3 = (bf16[1056,8,32]{0,2,1:T(8,128)(2,1)S(1)}, bf16[1056,8,32]{0,2,1:T(8,128)(2,1)}, u32[]{:S(2)}) copy-start(bf16[1056,8,32]{0,2,1:T(8,128)(2,1)} %reshape.286) | copy-start | bytes 1622020
  47.8 19.5 %copy-start.7 = (bf16[384,256]{0,1:T(8,128)(2,1)S(1)}, bf16[384,256]{0,1:T(8,128)(2,1)}, u32[]{:S(2)}) copy-start(bf16[384,256]{0,1:T(8,128)(2,1)} %copy-done.6) | copy-start | bytes 589828
  105.3 14.0 %collective-permute-start.4 = (f32[24,6,512]{2,1,0:T(8,128)}, f32[24,6,512]{2,1,0:T(8,128)}, u32[]{:S(2)}, u32[]{:S(2)}) collective-permute-start(f32[24,6,512]{2,1,0:T(8,128)} %fusion.31), channel_id=1, source_target_pairs={{0,7},{1,0},{2,1},{3,2},{4,3},{5,4},{6,5},{7,6},{8,15},{9,8},{10,9... | collective-permute-start | bytes 884744 | tf_op jit(solution)/shard_map/ppermute | solution.py:13
  118.3 30.1 %copy-start.1 = (bf16[12,32,256]{2,1,0:T(8,128)(2,1)S(1)}, bf16[12,32,256]{2,1,0:T(8,128)(2,1)}, u32[]{:S(2)}) copy-start(bf16[12,32,256]{2,1,0:T(8,128)(2,1)} %param.19) | copy-start | bytes 589828
  121.1 10.6 %collective-permute-start.5 = (f32[24,6,512]{2,1,0:T(8,128)}, f32[24,6,512]{2,1,0:T(8,128)}, u32[]{:S(2)}, u32[]{:S(2)}) collective-permute-start(f32[24,6,512]{2,1,0:T(8,128)} %get-tuple-element.98), channel_id=1, source_target_pairs={{0,1},{1,2},{2,3},{3,4},{4,5},{5,6},{6,7},{7,0},{8,9},{9,10},{10,1... | collective-permute-start | bytes 884744 | tf_op jit(solution)/shard_map/ppermute | solution.py:13
  122.5 37.0 %copy-start.4 = (bf16[256,256]{1,0:T(8,128)(2,1)S(1)}, bf16[256,256]{1,0:T(8,128)(2,1)}, u32[]{:S(2)}) copy-start(bf16[256,256]{1,0:T(8,128)(2,1)} %param.16) | copy-start | bytes 393220
  122.5 37.4 %copy-start.5 = (bf16[256,256]{1,0:T(8,128)(2,1)S(1)}, bf16[256,256]{1,0:T(8,128)(2,1)}, u32[]{:S(2)}) copy-start(bf16[256,256]{1,0:T(8,128)(2,1)} %param.17) | copy-start | bytes 393220
  137.6 17.7 %collective-permute-start.6 = (f32[6,32,512]{2,1,0:T(8,128)S(1)}, f32[6,32,512]{2,1,0:T(8,128)S(1)}, u32[]{:S(2)}, u32[]{:S(2)}) collective-permute-start(f32[6,32,512]{2,1,0:T(8,128)S(1)} %get-tuple-element.101), channel_id=1, source_target_pairs={{8,0},{16,8},{24,16},{32,24},{40,32},{48,40},{56,48},{64,56},{72,6... | collective-permute-start | bytes 1179656 | tf_op jit(solution)/shard_map/ppermute | solution.py:19
  150.2 6.6 %collective-permute-start.7 = (f32[6,32,512]{2,1,0:T(8,128)S(1)}, f32[6,32,512]{2,1,0:T(8,128)S(1)}, u32[]{:S(2)}, u32[]{:S(2)}) collective-permute-start(f32[6,32,512]{2,1,0:T(8,128)S(1)} %get-tuple-element.100), channel_id=1, source_target_pairs={{0,8},{8,16},{16,24},{24,32},{32,40},{40,48},{48,56},{56,64},{64,7... | collective-permute-start | bytes 1179656 | tf_op jit(solution)/shard_map/ppermute | solution.py:19
Sparse Core Ops, SparseCore 0:
  159.5 261.6 all-reduce.2
where the time goes:
time: 442 us; the launch traced here: 436 us
  waiting for transfers between devices  267 us (60%)
  matrix products  83.1 us (19%)
  local copies, waits for them, and re-layouts  32.3 us (7%)
  starting transfers between devices  27.1 us (6%)
  between operations  14.6 us (3%)
  other arithmetic  11.4 us (3%)
    psum x1, waiting for transfers between devices, body(): lax.psum((term_query, term_key, term_value, term_out), ('lat', 'lon'))  260 us
    dot_general x1, matrix products, window_block(): jnp.einsum('hqk,qhe->khe', grad_scores, query_heads, preferred_element_ty...  20.3 us
    dot_general x1, matrix products, window_block(): jnp.einsum('hqk,khe->qhe', grad_scores, key_heads, preferred_element_type...  19.5 us
    ppermute x2, starting transfers between devices, from_behind(): lax.ppermute(value, axis, [(source, source + steps) for source in range(l...  12.6 us
  transfers between devices with their start and end apart: 9, of which 5 were waited for; matrix products, arithmetic and copies ran while one was open for 7% of the time, Pallas kernels for 0%

commit v1 on v0

v1 whole, which is shorter than its diff:
```python
import functools

import jax
import jax.numpy as jnp
from jax import lax
from jax.experimental import pallas as pl
from jax.experimental.pallas import tpu as pltpu
from jax.sharding import PartitionSpec as P

HEADS = 8
REACH = 6
EDGE = 8
TILE_ROWS = 4
TILE_COLS = 8
MESH = pl.DeviceIdType.MESH
MOVES = [(a, b) for a in (-1, 0, 1) for b in (-1, 0, 1) if (a, b) != (0, 0)]
BF16 = jnp.bfloat16
F32 = jnp.float32
VMEM_SPEC = pl.BlockSpec(memory_space=pltpu.VMEM)


def nn(a, b):
    return lax.dot_general(a, b, (((1,), (0,)), ((), ())), preferred_element_type=F32)


def nt(a, b):
    return lax.dot_general(a, b, (((1,), (1,)), ((), ())), preferred_element_type=F32)


def tn(a, b):
    return lax.dot_general(a, b, (((0,), (0,)), ((), ())), preferred_element_type=F32)


def split(x):
    high = x.astype(BF16)
    return high, (x - high.astype(F32)).astype(BF16)


def span(move, inner, edge, outer):
    if move == 0:
        return pl.ds(0, inner), pl.ds(outer, inner), pl.ds(outer, inner)
    if move > 0:
        return pl.ds(inner - edge, edge), pl.ds(0, edge), pl.ds(outer + inner, edge)
    return pl.ds(0, edge), pl.ds(outer + inner, edge), pl.ds(0, edge)


def neighbour(a, b):
    n_lat, n_lon = lax.axis_size("lat"), lax.axis_size("lon")
    lat, lon = lax.axis_index("lat"), lax.axis_index("lon")
    return (lax.rem(lat + a + n_lat, n_lat), lax.rem(lon + b + n_lon, n_lon))


def halo_kernel(cells, ext, send, recv, own_sem):
    rows, cols = cells.shape[0], cells.shape[1]
    barrier = pltpu.get_barrier_semaphore()
    for a, b in MOVES:
        pl.semaphore_signal(barrier, inc=1, device_id=neighbour(a, b), device_id_type=MESH)
    own = pltpu.make_async_copy(cells, ext.at[pl.ds(REACH, rows), pl.ds(EDGE, cols)], own_sem)
    own.start()
    pl.semaphore_wait(barrier, len(MOVES))
    copies = []
    for n, (a, b) in enumerate(MOVES):
        row_from, row_to, _ = span(a, rows, REACH, REACH)
        col_from, col_to, _ = span(b, cols, EDGE, EDGE)
        copies.append(
            pltpu.make_async_remote_copy(
                src_ref=cells.at[row_from, col_from],
                dst_ref=ext.at[row_to, col_to],
                send_sem=send.at[n],
                recv_sem=recv.at[n],
                device_id=neighbour(a, b),
                device_id_type=MESH,
            )
        )
        copies[-1].start()
    own.wait()
    for copy in copies:
        copy.wait()


def attend_kernel(
    lat_rows,
    ext,
    cells,
    grad_out,
    wq,
    wk,
    wv,
    wo,
    mixed,
    own_grad,
    ext_grad,
    terms,
    qx,
    gx,
    kx,
    vx,
    ax,
    dqx,
    dkx,
    dvx,
    bias,
    heads_mask,
):
    rows, cols, width = cells.shape
    ext_rows, ext_cols, _ = ext.shape
    n_own, n_ext = rows * cols, ext_rows * ext_cols
    head_dim = width // HEADS
    k_rows, k_cols = TILE_ROWS + 2 * REACH, TILE_COLS + 2 * EDGE
    n_query, n_key = TILE_ROWS * TILE_COLS, k_rows * k_cols
    n_lane = HEADS * n_query
    scale = head_dim ** -0.5
    log2e = 1.4426950408889634

    ext_flat = ext[...].reshape(n_ext, width)
    kx[...] = nn(ext_flat, wk[...]).astype(BF16).astype(F32).reshape(kx.shape)
    vx[...] = nn(ext_flat, wv[...]).astype(BF16).astype(F32).reshape(vx.shape)
    cells_flat = cells[...].reshape(n_own, width)
    out_flat = grad_out[...].reshape(n_own, width)
    qx[...] = nn(cells_flat, wq[...]).astype(BF16).astype(F32).reshape(qx.shape)
    gx[...] = nt(out_flat, wo[...]).astype(BF16).astype(F32).reshape(gx.shape)
    dkx[...] = jnp.zeros_like(dkx)
    dvx[...] = jnp.zeros_like(dvx)

    lane_head = lax.broadcasted_iota(jnp.int32, (n_lane, width), 0) // n_query
    feature_head = lax.broadcasted_iota(jnp.int32, (n_lane, width), 1) // head_dim
    heads_mask[...] = jnp.where(lane_head == feature_head, 1.0, 0.0)

    shape4 = (k_rows, k_cols, n_lane)
    key_row = lax.broadcasted_iota(jnp.int32, shape4, 0)
    key_col = lax.broadcasted_iota(jnp.int32, shape4, 1)
    query = lax.broadcasted_iota(jnp.int32, shape4, 2) % n_query
    row_gap = key_row - query // TILE_COLS
    col_gap = key_col - query % TILE_COLS - (EDGE - REACH)
    inside = (row_gap >= 0) & (row_gap <= 2 * REACH) & (col_gap >= 0) & (col_gap <= 2 * REACH)
    lat_first = lax.axis_index("lat") * rows - REACH
    for i in range(rows // TILE_ROWS):
        lat_row = key_row + (lat_first + i * TILE_ROWS)
        ok = inside & (lat_row >= 0) & (lat_row < lat_rows)
        bias[i] = jnp.where(ok, 0.0, -1e30).reshape(n_key, n_lane)

    col_tiles = cols // TILE_COLS

    def one_tile(t, carry):
        i, j = t // col_tiles, t % col_tiles
        row0 = i * TILE_ROWS
        col0 = pl.multiple_of(j * TILE_COLS, TILE_COLS)
        at_query = (pl.ds(row0, TILE_ROWS), pl.ds(col0, TILE_COLS))
        at_key = (pl.ds(row0, k_rows), pl.ds(col0, k_cols))
        mask = heads_mask[...]
        q_tile = qx[at_query].reshape(n_query, width)
        g_tile = gx[at_query].reshape(n_query, width)
        q_heads = (jnp.concatenate([q_tile] * HEADS, axis=0) * mask).astype(BF16)
        g_heads = (jnp.concatenate([g_tile] * HEADS, axis=0) * mask).astype(BF16)
        k_tile = kx[at_key].reshape(n_key, width).astype(BF16)
        v_tile = vx[at_key].reshape(n_key, width).astype(BF16)
        scores = nt(k_tile, q_heads) * (scale * log2e) + bias[i]
        top = jnp.max(scores, axis=0, keepdims=True)
        weights = jnp.exp2(scores - top)
        weights = weights * (1.0 / jnp.sum(weights, axis=0, keepdims=True))
        low = weights.astype(BF16)
        grad_weights = nt(v_tile, g_heads)
        centre = jnp.sum(weights * grad_weights, axis=0, keepdims=True)
        grad_scores = (weights * (grad_weights - centre) * scale).astype(BF16)
        att = jnp.sum((tn(low, v_tile) * mask).reshape(HEADS, n_query, width), axis=0)
        dq = jnp.sum((tn(grad_scores, k_tile) * mask).reshape(HEADS, n_query, width), axis=0)
        tile_shape = (TILE_ROWS, TILE_COLS, width)
        ax[at_query] = att.astype(BF16).astype(F32).reshape(tile_shape)
        dqx[at_query] = dq.reshape(tile_shape)
        dkx[at_key] += nn(grad_scores, q_heads).reshape(k_rows, k_cols, width)
        dvx[at_key] += nn(low, g_heads).reshape(k_rows, k_cols, width)
        return carry

    lax.fori_loop(0, (rows // TILE_ROWS) * col_tiles, one_tile, 0)

    att = ax[...].reshape(n_own, width).astype(BF16)
    mixed[...] = nn(att, wo[...]).astype(BF16).reshape(mixed.shape)
    terms[pl.ds(3 * width, width)] = tn(att, out_flat)
    q_high, q_low = split(dqx[...].reshape(n_own, width))
    cells_t = cells_flat.T
    terms[pl.ds(0, width)] = nn(cells_t, q_high) + nn(cells_t, q_low)
    own_query = nt(q_high, wq[...]) + nt(q_low, wq[...])
    ext_t = ext_flat.T
    k_high, k_low = split(dkx[...].reshape(n_ext, width))
    v_high, v_low = split(dvx[...].reshape(n_ext, width))
    terms[pl.ds(width, width)] = nn(ext_t, k_high) + nn(ext_t, k_low)
    terms[pl.ds(2 * width, width)] = nn(ext_t, v_high) + nn(ext_t, v_low)
    back = nt(k_high, wk[...]) + nt(k_low, wk[...]) + nt(v_high, wv[...]) + nt(v_low, wv[...])
    kx[...] = back.reshape(kx.shape)
    ext_grad[...] = back.astype(BF16).reshape(ext_grad.shape)
    own_grad[...] = (
        kx[pl.ds(REACH, rows), pl.ds(EDGE, cols), :] + own_query.reshape(own_grad.shape)
    )


def total_kernel(
    chips,
    depth,
    terms,
    ext_grad,
    gathered,
    *refs,
):
    rims = refs[: len(MOVES)]
    (
        pair_in,
        plane_out,
        plane_in,
        column_out,
        column_in,
        result,
        rim_sems,
        pair_sems,
        plane_send,
        plane_recv,
        column_send,
        column_recv,
        spread_send,
        spread_recv,
        relay_send,
        relay_recv,
        self_sem,
    ) = refs[len(MOVES) :]
    lat, lon = lax.axis_index("lat"), lax.axis_index("lon")
    n_lon = lax.axis_size("lon")
    per_plane = chips // n_lon
    core = lat % 2
    x_lo = (lat // 2) % per_plane
    z = lat // (2 * per_plane)
    me = x_lo * n_lon + lon
    partner = (lat + 1 - 2 * core, lon)

    def plane_peer(p):
        return ((z * per_plane + p // n_lon) * 2 + core, p % n_lon)

    def column_peer(w):
        return ((w * per_plane + x_lo) * 2 + core, lon)

    barrier = pltpu.get_barrier_semaphore()

    def greet(device):
        pl.semaphore_signal(barrier, inc=1, device_id=device, device_id_type=MESH)

    greet(partner)
    for step in range(1, chips):
        greet(plane_peer((me + step) % chips))
    for step in range(1, depth):
        greet(column_peer((z + step) % depth))
    for a, b in MOVES:
        greet(neighbour(a, b))
    pl.semaphore_wait(barrier, 1 + (chips - 1) + (depth - 1) + len(MOVES))

    def remote(src, dst, send, recv, device):
        return pltpu.make_async_remote_copy(
            src_ref=src,
            dst_ref=dst,
            send_sem=send,
            recv_sem=recv,
            device_id=device,
            device_id_type=MESH,
        )

    pair = remote(terms.at[1 - core], pair_in, pair_sems.at[0], pair_sems.at[1], partner)
    pair.start()
    rim_copies = []
    rows = ext_grad.shape[0] - 2 * REACH
    cols = ext_grad.shape[1] - 2 * EDGE
    for n, (a, b) in enumerate(MOVES):
        _, _, row_from = span(a, rows, REACH, REACH)
        _, _, col_from = span(b, cols, EDGE, EDGE)
        rim_copies.append(
            remote(
                ext_grad.at[row_from, col_from],
                rims[n],
                rim_sems.at[0, n],
                rim_sems.at[1, n],
                neighbour(a, b),
            )
        )
        rim_copies[-1].start()
    pair.wait()
    plane_out[...] = (terms[core] + pair_in[...]).astype(BF16)
    plane_in[me] = plane_out[me]
    copies = []
    for step in range(1, chips):
        to = (me + step) % chips
        copies.append(
            remote(
                plane_out.at[to],
                plane_in.at[me],
                plane_send.at[step],
                plane_recv.at[step],
                plane_peer(to),
            )
        )
        copies[-1].start()
    for copy in copies:
        copy.wait()
    column_out[...] = jnp.sum(plane_in[...].astype(F32), axis=0)
    column_in[z] = column_out[...]
    copies = []
    for step in range(1, depth):
        to = (z + step) % depth
        copies.append(
            remote(
                column_out,
                column_in.at[z],
                column_send.at[step],
                column_recv.at[step],
                column_peer(to),
            )
        )
        copies[-1].start()
    for copy in copies:
        copy.wait()
    result[...] = jnp.sum(column_in[...], axis=0).astype(BF16)
    copies = []
    own = pltpu.make_async_copy(result, gathered.at[core, me], self_sem)
    own.start()
    for step in range(1, chips):
        to = (me + step) % chips
        copies.append(
            remote(
                result,
                gathered.at[core, me],
                spread_send.at[step],
                spread_recv.at[step],
                plane_peer(to),
            )
        )
        copies[-1].start()
    relays = [
        remote(result, gathered.at[core, me], relay_send.at[0], relay_recv.at[0], partner)
    ]
    relays[0].start()
    for step in range(1, chips):
        copies[step - 1].wait_recv()
        come = (me - step + chips) % chips
        relays.append(
            remote(
                gathered.at[core, come],
                gathered.at[core, come],
                relay_send.at[step],
                relay_recv.at[step],
                partner,
            )
        )
        relays[-1].start()
    own.wait()
    for copy in copies:
        copy.wait_send()
    for relay in relays:
        relay.wait()
    for copy in rim_copies:
        copy.wait()


def finish_kernel(grad_scale, own_grad, gathered, *refs):
    rims = refs[: len(MOVES)]
    grad_cells, *weight_grads = refs[len(MOVES) :]
    rows, cols, width = own_grad.shape
    grad_cells[...] = own_grad[...]
    for n, (a, b) in enumerate(MOVES):
        row_at = (pl.ds(0, rows), pl.ds(0, REACH), pl.ds(rows - REACH, REACH))[a]
        col_at = (pl.ds(0, cols), pl.ds(0, EDGE), pl.ds(cols - EDGE, EDGE))[b]
        grad_cells[row_at, col_at, :] += rims[n][...].astype(F32)
    for n, out in enumerate(weight_grads):
        out[...] = gathered[pl.ds(n * width, width), :].astype(F32) * grad_scale


def call(kernel, outs, count, scratch, **params):
    return pl.pallas_call(
        kernel,
        out_shape=outs,
        in_specs=[VMEM_SPEC] * count,
        out_specs=jax.tree.map(lambda _: VMEM_SPEC, outs),
        scratch_shapes=scratch,
        compiler_params=pltpu.CompilerParams(**params),
    )


def body(cells, w_query, w_key, w_value, w_out, grad_out):
    rows, cols, width = cells.shape
    n_lat, n_lon = lax.axis_size("lat"), lax.axis_size("lon")
    ext_rows, ext_cols = rows + 2 * REACH, cols + 2 * EDGE
    shape = jax.ShapeDtypeStruct
    dma = pltpu.SemaphoreType.DMA

    ext = call(
        halo_kernel,
        shape((ext_rows, ext_cols, width), BF16),
        1,
        [dma((len(MOVES),)), dma((len(MOVES),)), dma],
        collective_id=0,
        has_side_effects=True,
    )(cells)

    own_shape, ext_shape = (rows, cols, width), (ext_rows, ext_cols, width)
    n_query = TILE_ROWS * TILE_COLS
    n_key = (TILE_ROWS + 2 * REACH) * (TILE_COLS + 2 * EDGE)
    mixed, own_grad, ext_grad, terms = call(
        functools.partial(attend_kernel, rows * n_lat),
        (
            shape(own_shape, BF16),
            shape(own_shape, F32),
            shape(ext_shape, BF16),
            shape((4 * width, width), F32),
        ),
        7,
        [pltpu.VMEM(own_shape, F32)] * 2
        + [pltpu.VMEM(ext_shape, F32)] * 2
        + [pltpu.VMEM(own_shape, F32)] * 2
        + [pltpu.VMEM(ext_shape, F32)] * 2
        + [
            pltpu.VMEM((rows // TILE_ROWS, n_key, HEADS * n_query), F32),
            pltpu.VMEM((HEADS * n_query, width), F32),
        ],
        vmem_limit_bytes=60 * 1024 * 1024,
    )(ext, cells, grad_out, w_query, w_key, w_value, w_out)

    chips, depth = 16, n_lat * n_lon // 32
    chunk = 2 * width // chips
    rim_shapes = tuple(
        shape((rows if a == 0 else REACH, cols if b == 0 else EDGE, width), BF16)
        for a, b in MOVES
    )
    gathered, *rims = call(
        functools.partial(total_kernel, chips, depth),
        (shape((2, chips, chunk, width), BF16),) + rim_shapes,
        2,
        [
            pltpu.VMEM((chips, chunk, width), F32),
            pltpu.VMEM((chips, chunk, width), BF16),
            pltpu.VMEM((chips, chunk, width), BF16),
            pltpu.VMEM((chunk, width), F32),
            pltpu.VMEM((depth, chunk, width), F32),
            pltpu.VMEM((chunk, width), BF16),
            dma((2, len(MOVES))),
            dma((2,)),
            dma((chips,)),
            dma((chips,)),
            dma((depth,)),
            dma((depth,)),
            dma((chips,)),
            dma((chips,)),
            dma((chips,)),
            dma((chips,)),
            dma,
        ],
        collective_id=1,
        has_side_effects=True,
    )(terms.reshape(2, chips, chunk, width), ext_grad)

    grad_scale = (rows * n_lat * cols * n_lon) ** -0.5
    grad_cells, grad_wq, grad_wk, grad_wv, grad_wo = call(
        functools.partial(finish_kernel, grad_scale),
        (shape(own_shape, F32),) + (shape((width, width), F32),) * 4,
        2 + len(MOVES),
        [],
    )(own_grad, gathered.reshape(4 * width, width), *rims)
    return mixed, grad_cells, grad_wq, grad_wk, grad_wv, grad_wo


def solution(mesh):
    in_specs = (P("lat", "lon", None), P(), P(), P(), P(), P("lat", "lon", None))
    out_specs = (P("lat", "lon", None), P("lat", "lon", None), P(), P(), P(), P())
    return jax.shard_map(body, mesh=mesh, in_specs=in_specs, out_specs=out_specs, check_vma=False)
```

time: 442 us -> 72.9 us (0.16); the launches traced: 436 us -> 72.7 us
  waiting for transfers between devices: 267 us -> 0 us
  matrix products: 83.1 us -> 0 us
  Pallas kernels: 0 us -> 72.1 us
  local copies, waits for them, and re-layouts: 32.3 us -> 0 us
  starting transfers between devices: 27.1 us -> 0 us
  between operations: 14.6 us -> 0.65 us
  other arithmetic: 11.4 us -> 0 us
    psum x1 -> x0, waiting for transfers between devices: 260 us -> none  [body(): lax.psum((term_query, term_key, term_value, term_out), ('lat', 'lon'))]
    dot_general x16 -> x0, matrix products: 74.5 us -> none  [the longest x1 20.3 us: window_block(): jnp.einsum('hqk,qhe->khe', grad_scores, query_heads, preferred_element_ty...]
    pallas_call x0 -> x4, Pallas kernels: none -> 72.1 us  [the longest x1 36 us: body(): call(functools.partial(total_kernel, chips, depth), (shape((2, chips, chu...]
    ppermute x8 -> x0, starting transfers between devices: 27 us -> none  [the longest x2 12.6 us: from_behind(): lax.ppermute(value, axis, [(source, source + steps) for source in range(l...]
    reshape x6 -> x0, local copies, waits for them, and re-layouts: 12.6 us -> none  [the longest x2 4.98 us: window_block(): grad_value.reshape(k_rows, k_cols, model_width)]
    sub x1 -> x0, matrix products: 8.58 us -> none  [window_block(): weights = jnp.exp(scores - row_max)]
    ppermute x8 -> x0, waiting for transfers between devices: 6.93 us -> none  [the longest x2 4.79 us: passed_along(): return lax.ppermute(value, axis, pairs)]
    scatter-add x2 -> x0, local copies, waits for them, and re-layouts: 6.5 us -> none  [the longest x1 3.55 us: return_rim(): folded = folded.at[:, :REACH].add(arrived)]
  transfers between devices with their start and end apart: 9 -> 0, of which waited for: 5 -> 0; matrix products, arithmetic and copies ran while one was open for 7% -> 0% of each run, Pallas kernels for 0% -> 0%
where the time goes in v1:
time: 72.9 us; the launch traced here: 72.7 us
  Pallas kernels  72.1 us (99%)
    pallas_call x1, Pallas kernels, body(): call(functools.partial(total_kernel, chips, depth), (shape((2, chips, chu...  36 us
    pallas_call x1, Pallas kernels, body(): call(halo_kernel, shape((ext_rows, ext_cols, width), BF16), 1, [dma((len(...  17 us
    pallas_call x1, Pallas kernels, body(): call(functools.partial(attend_kernel, rows * n_lat), (shape(own_shape, BF...  16.6 us
    pallas_call x1, Pallas kernels, body(): call(functools.partial(finish_kernel, grad_scale), (shape(own_shape, F32)...  2.4 us

profile of v1, /device:TPU:1, one launch (start us, length us, event | category | flops | bytes accessed | tf_op | source)
XLA Modules:
  0.0 72.7 jit_solution(2724004825926172932)
XLA Ops:
  0.6 17.0 %shard_map.109.ext = bf16[24,48,256]{2,1,0:T(8,128)(2,1)} custom-call(bf16[12,32,256]{2,1,0:T(8,128)(2,1)} %cells.3), custom_call_target="tpu_custom_call" | custom-call | tf_op jit(solution)/shard_map/pallas_call | solution.py:389
  17.7 16.6 %shard_map.110 = (bf16[12,32,256]{2,1,0:T(8,128)(2,1)}, f32[12,32,256]{2,1,0:T(8,128)}, bf16[24,48,256]{2,1,0:T(8,128)(2,1)}, f32[1024,256]{1,0:T(8,128)}) custom-call(bf16[24,48,256]{2,1,0:T(8,128)(2,1)} %shard_map.109.ext, bf16[12,32,256]{2,1,0:T(8,128)(2,1)} %cells.3, bf16[12,32,256]{2,1,0:T(8,128)(2,1)} %grad_out.1, bf16[256,256]{1,0:T(8,128)(2,1)} %wq.1, ...), custom_call_target="tpu_custom_call" | custom-call | tf_op jit(solution)/shard_map/pallas_call | solution.py:401
  34.3 36.0 %shard_map.111 = (bf16[2,16,32,256]{3,2,1,0:T(8,128)(2,1)}, bf16[6,8,256]{2,1,0:T(8,128)(2,1)}, bf16[6,32,256]{2,1,0:T(8,128)(2,1)}, bf16[6,8,256]{2,1,0:T(8,128...) custom-call(f32[2,16,32,256]{3,2,1,0:T(8,128)} %bitcast.2, ...), custom_call_target="tpu_custom_call" | custom-call | tf_op jit(solution)/shard_map/pallas_call | solution.py:427
  70.3 2.4 %shard_map.112 = (f32[12,32,256]{2,1,0:T(8,128)}, f32[256,256]{1,0:T(8,128)}, f32[256,256]{1,0:T(8,128)}, f32[256,256]{1,0:T(8,128)}, f32[256,256]{1,0:T(8,128)}) custom-call(f32[12,32,256]{2,1,0:T(8,128)} %get-tuple-element.25.own_grad, bf16[1024,256]{1,0:T(8,128)(2,1)} %bitcast.3, bf16[6,8,256]{2,1,0:T(8,128)(2,1)} %get-tuple-element.29.refs_0_, ...), custom_call_target="tpu_custom_call" | custom-call | tf_op jit(solution)/shard_map/pallas_call | solution.py:455
